TPU v7x, 32 devices: a whole 2x2x4 slice. The times are simulated.
32 devices in a mesh: parts: 2 (over y), blk: 16 (over z, x, core).
Axes of the slice: x: 2, y: 2, z: 4, core: 2. Of those that a mesh axis runs over, the one named last changes fastest.
Arguments:
- features: bfloat16 [8192, 128], P(('parts', 'blk')), parts along dimension 0, may hold values from -6 to 6
- w_first: bfloat16 [128, 256], replicated, may hold values from -0.5 to 0.5
- w_second: bfloat16 [256, 8192], replicated, may hold values from -0.375 to 0.375
- panel: bfloat16 [64, 64, 256], P(('parts', 'blk')), parts along dimension 0, may hold values from -6 to 6
- energies: float32 [256], replicated, may hold values from -1 to 1
- pair_dest: int32 [8192, 1], P(('parts', 'blk')), parts along dimension 0, may hold values from 0 to 15, as said below
- pair_row: int32 [8192], P(('parts', 'blk')), parts along dimension 0, may hold values from 0 to 1
- pair_col: int32 [8192], P(('parts', 'blk')), parts along dimension 0, may hold values from 0 to 1
Outputs:
- residual: float32 [64, 64, 256], P(('parts', 'blk')), parts along dimension 0
- loss: float32 [2], P('parts'), parts along dimension 0
- grad_first: float32 [256, 256], P('parts'), parts along dimension 0
- grad_second: float32 [512, 8192], P('parts', 'blk'), parts along dimension 0
There are 2 independent parts, one for each index of `parts`. A program takes and returns all parts, laid end to end along the dimension named above; an argument that names none is the same for every part. Nothing has to cross between parts.
Inputs may be any that keep to these rules, and one draw needn't show every extreme that they name: `pair_dest`: among one device's 256 pairs at most 24 have their block row on one device; every device owns the block rows of exactly 24 of its own pairs. Owners lie mostly near the listing device along the axis.
All inputs are finite; a program needn't handle non-finite values.
Results may differ from a plain program's by a relative error of at most 0.004.
Values may be sent and summed in bfloat16 or wider, within the bound.
No kernel may reach another device: no remote copies, remote signals or barrier semaphores. Data moves between devices by JAX's collectives and lax.ppermute only.
A program may use at most 128 MiB of HBM per device.

v0:
```python
import jax
import jax.numpy as jnp
from jax import lax
from jax.sharding import PartitionSpec as P


def predict(feats, w_first, w_second, orbitals):
    pre = jnp.dot(feats, w_first, preferred_element_type=jnp.float32)
    hidden = jax.nn.silu(pre).astype(jnp.bfloat16)
    blocks = (jnp.dot(hidden, w_second, preferred_element_type=jnp.float32) / orbitals).astype(
        jnp.bfloat16
    )
    return (pre, hidden, blocks)


def weight_terms(feats, pre, hidden, d_flat, w_second, orbitals):
    term_second = jnp.dot(hidden.T, d_flat, preferred_element_type=jnp.float32) / orbitals
    d_hidden = (
        lax.dot_general(
            d_flat, w_second, (((1,), (1,)), ((), ())), preferred_element_type=jnp.float32
        )
        / orbitals
    )
    sig = jax.nn.sigmoid(pre)
    d_pre = (d_hidden * sig * (1.0 + pre * (1.0 - sig))).astype(jnp.bfloat16)
    term_first = jnp.dot(feats.T, d_pre, preferred_element_type=jnp.float32)
    return (term_first, term_second)


def slot_work(slot_blocks, slot_panel, slot_rows, energies, blk_dev, total_blocks):
    slots, unused_two, orbitals, unused_o = slot_blocks.shape
    columns = slot_panel.shape[2]
    group = 32
    steps_count = slots // group
    grouped = (
        slot_blocks.reshape(steps_count, group, 2, orbitals, orbitals),
        slot_panel.reshape(steps_count, group, orbitals, columns),
        slot_rows.reshape(steps_count, group),
    )
    row_ids = jnp.arange(blk_dev, dtype=jnp.int32)

    def forward(total, item):
        blocks, coeffs, rows = item
        h_panel = jnp.einsum(
            "sab,sbp->sap", blocks[:, 0], coeffs, preferred_element_type=jnp.float32
        )
        s_panel = jnp.einsum(
            "sab,sbp->sap", blocks[:, 1], coeffs, preferred_element_type=jnp.float32
        )
        contrib = h_panel - s_panel * energies
        selector = (rows[None, :] == row_ids[:, None]).astype(jnp.float32)
        added = jnp.einsum("rs,sap->rap", selector, contrib, precision=lax.Precision.HIGHEST)
        return (total + added, None)

    residual = lax.scan(forward, jnp.zeros((blk_dev, orbitals, columns), jnp.float32), grouped)[0]
    grad_h = (residual / total_blocks).astype(jnp.bfloat16)
    grad_s = (-(residual * energies) / total_blocks).astype(jnp.bfloat16)

    def backward(carry, item):
        blocks, coeffs, rows = item
        valid = (rows >= 0)[:, None, None]
        safe_rows = jnp.maximum(rows, 0)
        gh_rows = jnp.where(valid, grad_h[safe_rows], jnp.zeros((), jnp.bfloat16))
        gs_rows = jnp.where(valid, grad_s[safe_rows], jnp.zeros((), jnp.bfloat16))
        d_h = jnp.einsum(
            "sap,sbp->sab", gh_rows, coeffs, preferred_element_type=jnp.float32
        ).astype(jnp.bfloat16)
        d_s = jnp.einsum(
            "sap,sbp->sab", gs_rows, coeffs, preferred_element_type=jnp.float32
        ).astype(jnp.bfloat16)
        return (carry, jnp.stack([d_h, d_s], axis=1))

    d_blocks = lax.scan(backward, 0, grouped)[1]
    return (residual, d_blocks.reshape(slots, 2, orbitals, orbitals))


def local(features, w_first, w_second, panel, energies, pair_dest, pair_row, pair_col):
    n_dev = lax.axis_size("blk")
    my_index = lax.axis_index("blk")
    pair_count, feat_width = features.shape
    blk_dev, orbitals, columns = panel.shape
    capacity = 3 * pair_count // (2 * n_dev)
    slots = n_dev * capacity
    total_blocks = blk_dev * n_dev
    dest = pair_dest[:, 0]
    dest_table = (dest[:, None] == jnp.arange(n_dev, dtype=jnp.int32)[None, :]).astype(jnp.int32)
    rank_in = jnp.sum(jnp.cumsum(dest_table, axis=0) * dest_table, axis=1) - 1
    slot_of = dest * capacity + rank_in
    source = (
        jnp.full((slots,), pair_count, jnp.int32)
        .at[slot_of]
        .set(jnp.arange(pair_count, dtype=jnp.int32))
    )
    empty_label = jnp.full((1,), -1, jnp.int32)
    rows_sent = jnp.concatenate([pair_row, empty_label])[source]
    cols_sent = jnp.concatenate([my_index * blk_dev + pair_col, jnp.zeros((1,), jnp.int32)])[source]
    labels = jnp.stack([rows_sent, cols_sent], axis=-1).reshape(n_dev, capacity, 2)
    whole_panel = lax.all_gather(panel, "blk", axis=0, tiled=True)
    pre, hidden, blocks = predict(features, w_first, w_second, orbitals)
    padded = jnp.concatenate([blocks, jnp.zeros((1, blocks.shape[1]), jnp.bfloat16)], axis=0)
    send_blocks = padded[source].reshape(n_dev, capacity, 2, orbitals, orbitals)
    got_blocks, got_labels = (
        lax.all_to_all(send_blocks, "blk", split_axis=0, concat_axis=0, tiled=True),
        lax.all_to_all(labels, "blk", split_axis=0, concat_axis=0, tiled=True),
    )
    got_labels = got_labels.reshape(slots, 2)
    slot_panel = whole_panel[got_labels[:, 1]]
    residual, d_blocks = slot_work(
        got_blocks.reshape(slots, 2, orbitals, orbitals),
        slot_panel,
        got_labels[:, 0],
        energies,
        blk_dev,
        total_blocks,
    )
    back = lax.all_to_all(
        d_blocks.reshape(n_dev, capacity, 2, orbitals, orbitals),
        "blk",
        split_axis=0,
        concat_axis=0,
        tiled=True,
    )
    d_flat = back.reshape(slots, 2 * orbitals * orbitals)[slot_of]
    term_first, term_second = weight_terms(features, pre, hidden, d_flat, w_second, orbitals)
    grad_second = lax.psum_scatter(term_second, "blk", scatter_dimension=1, tiled=True)
    grad_first, square_sum = lax.psum((term_first, jnp.sum(residual * residual)), "blk")
    loss = (square_sum / (total_blocks * orbitals * columns)).reshape(1)
    return (residual, loss, grad_first, grad_second)


def solution(mesh):
    in_specs = (
        P(("parts", "blk"), None),
        P(),
        P(),
        P(("parts", "blk"), None, None),
        P(),
        P(("parts", "blk"), None),
        P(("parts", "blk")),
        P(("parts", "blk")),
    )
    out_specs = (P(("parts", "blk"), None, None), P("parts"), P("parts", None), P("parts", "blk"))
    return jax.shard_map(local, mesh=mesh, in_specs=in_specs, out_specs=out_specs, check_vma=False)
```

profile of v0, /device:TPU:0, one launch (start us, length us, event | category | flops | bytes accessed | tf_op | source)
XLA Modules:
  0.0 824.7 jit_solution(7765582669645620948)
XLA Ops:
  12.3 2.8 gather_fusion.3
  19.4 7.4 all-to-all-start
  27.8 3.5 fusion.35
  33.7 17.6 %gather_fusion.4 = bf16[384,8192]{1,0:T(8,128)(2,1)} fusion(bf16[257,8192]{1,0:T(8,128)(2,1)} %concatenate.12, s32[1024]{0:T(1024)S(1)} %pad_clamp_fusion.3), kind=kCustom, calls=%fused_computation.4 | custom fusion | bytes 12584448 | tf_op jit(solution)/shard_map/gather | solution.py:101
  51.4 17.9 %reshape.77 = bf16[16,24,2,64,64]{4,3,2,1,0:T(8,128)(2,1)} reshape(bf16[384,8192]{1,0:T(8,128)(2,1)} %gather_fusion.4) | data formatting | bytes 12582912 | tf_op jit(solution)/shard_map/reshape | solution.py:101
  69.2 16.7 %reshape.156 = bf16[16,2,98304]{2,1,0:T(2,128)(2,1)} reshape(bf16[16,24,2,64,64]{4,3,2,1,0:T(8,128)(2,1)} %reshape.77) | data formatting | bytes 12582912
  85.9 6.0 all-to-all-start.1
  92.9 98.0 %all-gather.2.cloned.1.call-done = bf16[32,64,256]{2,1,0:T(8,128)(2,1)} async-done(((bf16[2,64,256]{2,1,0:T(8,128)(2,1)}), bf16[32,64,256]{2,1,0:T(8,128)(2,1)}) %all-gather.2.cloned.1.call-update) | async-done | bytes 1048592 | tf_op jit(solution)/shard_map/all_gather | solution.py:98
  191.0 12.4 %gather_fusion.5 = bf16[384,64,256]{2,1,0:T(8,128)(2,1)} fusion(bf16[32,64,256]{2,1,0:T(8,128)(2,1)} %all-gather.2.cloned.1.call-done, s32[1024]{0:T(1024)S(1)} %pad_clamp_fusion.2), kind=kCustom, calls=%fused_computation.5 | custom fusion | bytes 25167360 | tf_op jit(solution)/shard_map/gather | solution.py:107
  203.4 9.2 %all-to-all-done.1 = bf16[16,2,98304]{2,1,0:T(2,128)(2,1)} async-done(((bf16[16,2,98304]{2,1,0:T(2,128)(2,1)}), bf16[16,2,98304]{2,1,0:T(2,128)(2,1)}, u32[]{:S(2)}, u32[]{:S(2)}) %all-to-all-start.1) | async-done | bytes 6291488 | tf_op jit(solution)/shard_map/all_to_all | solution.py:103
  212.5 16.4 %reshape.157 = bf16[16,24,2,64,64]{4,3,2,1,0:T(8,128)(2,1)} reshape(bf16[16,2,98304]{2,1,0:T(2,128)(2,1)} %all-to-all-done.1) | data formatting | bytes 12582912
  229.0 82.3 %while.22 = (s32[]{:T(128)}, f32[2,64,256]{2,0,1:T(2,128)S(1)}, s32[12,32]{1,0:T(8,128)S(1)}, bf16[12,32,2,64,64]{4,3,2,1,0:T(8,128)(2,1)}, bf16[12,32,64,256]{3...) while((s32[]{:T(128)}, f32[2,64,256]{2,0,1:T(2,128)S(1)}, ...), condition=%wide.region_5.6_spmd.clone, body=%wide.region_4.5_spmd.clone.sunk | while | flops 147914816 | bytes 13372387 | solution.py:55
  312.1 72.8 %while.21 = (s32[]{:T(128)}, bf16[12,32,2,64,64]{4,3,2,1,0:T(8,128)(2,1)}, s32[12,32]{1,0:T(8,128)S(1)}, bf16[2,64,256]{2,1,0:T(8,128)(2,1)S(1)}, bf16[12,32,64,...) while((s32[]{:T(128)}, bf16[12,32,2,64,64]{4,3,2,1,0:T(8,128)(2,1)}, ...), condition=%wide.region_9.10_spmd, body=%wide.region_8.9_spmd.sunk | while | flops 135791680 | bytes 10492341 | solution.py:73
  384.8 16.6 %reshape.158 = bf16[16,2,98304]{2,1,0:T(2,128)(2,1)} reshape(bf16[16,24,2,64,64]{4,3,2,1,0:T(8,128)(2,1)} %bitcast.100) | data formatting | bytes 12582912
  401.5 28.0 %all-to-all-start.2 = ((bf16[16,2,98304]{2,1,0:T(2,128)(2,1)}), bf16[16,2,98304]{2,1,0:T(2,128)(2,1)}, u32[]{:S(2)}, u32[]{:S(2)}) async-start(bf16[16,2,98304]{2,1,0:T(2,128)(2,1)} %reshape.158), calls=%async_computation.2 | async-start | bytes 12582912 | tf_op jit(solution)/shard_map/all_to_all | solution.py:116
  429.9 113.9 %all-to-all-done.2 = bf16[16,2,98304]{2,1,0:T(2,128)(2,1)} async-done(((bf16[16,2,98304]{2,1,0:T(2,128)(2,1)}), bf16[16,2,98304]{2,1,0:T(2,128)(2,1)}, u32[]{:S(2)}, u32[]{:S(2)}) %all-to-all-start.2) | async-done | bytes 6291488 | tf_op jit(solution)/shard_map/all_to_all | solution.py:116
  543.7 16.3 %reshape.159 = bf16[16,24,2,64,64]{4,3,2,1,0:T(8,128)(2,1)} reshape(bf16[16,2,98304]{2,1,0:T(2,128)(2,1)} %all-to-all-done.2) | data formatting | bytes 12582912
  560.0 17.0 %reshape.80 = bf16[384,8192]{1,0:T(8,128)(2,1)} reshape(bf16[16,24,2,64,64]{4,3,2,1,0:T(8,128)(2,1)} %reshape.159) | data formatting | bytes 12582912 | tf_op jit(solution)/shard_map/reshape | solution.py:123
  577.0 12.6 %gather_fusion.6 = bf16[256,8192]{1,0:T(8,128)(2,1)} fusion(bf16[384,8192]{1,0:T(8,128)(2,1)} %reshape.80, s32[1024]{0:T(1024)S(1)} %pad_clamp_fusion.1), kind=kCustom, calls=%fused_computation.6 | custom fusion | bytes 8389632 | tf_op jit(solution)/shard_map/gather | solution.py:123
  589.6 5.7 convolution_bitcast_fusion
  595.3 6.7 convolution_multiply_fusion
  602.1 56.7 %psum.14 = f32[]{:T(128)} all-reduce(f32[]{:T(128)} %get-tuple-element.172), channel_id=1, replica_groups=mesh['parts'=2,'blk'=16] {'blk'}, use_global_device_ids=true, to_apply=%region_7.8 | all-reduce | flops 1 | bytes 8 | tf_op jit(solution)/shard_map/psum | solution.py:126
  660.1 45.8 %all-reduce.3.cloned.1.call-done = f32[128,256]{0,1:T(8,128)} async-done(((f32[128,256]{0,1:T(8,128)}), f32[128,256]{0,1:T(8,128)}) %all-reduce.3.cloned.1.call-update) | async-done | bytes 131088 | tf_op jit(solution)/shard_map/psum | solution.py:126
  707.6 109.5 %reduce-scatter.2.cloned.1.call-done = f32[256,512]{1,0:T(8,128)} async-done(((f32[256,8192]{1,0:T(8,128)}), f32[256,512]{1,0:T(8,128)}) %reduce-scatter.2.cloned.1.call-update) | async-done | bytes 524304 | tf_op jit(solution)/shard_map/reduce_scatter | solution.py:125
  (201 shorter events, 171.4 us)
Async XLA Ops:
  7.2 19.6 %copy-start = (bf16[256,128]{1,0:T(8,128)(2,1)S(1)}, bf16[256,128]{1,0:T(8,128)(2,1)}, u32[]{:S(2)}) copy-start(bf16[256,128]{1,0:T(8,128)(2,1)} %param.12) | copy-start | bytes 196612
  19.4 66.5 %all-to-all-start = ((s32[16,24,2]{1,2,0:T(2,128)}), s32[16,24,2]{1,2,0:T(2,128)S(1)}, u32[]{:S(2)}, u32[]{:S(2)}) async-start(s32[16,24,2]{1,2,0:T(2,128)} %pad_add_fusion), calls=%async_computation | async-start | bytes 32768 | tf_op jit(solution)/shard_map/all_to_all | solution.py:104
  85.9 126.6 %all-to-all-start.1 = ((bf16[16,2,98304]{2,1,0:T(2,128)(2,1)}), bf16[16,2,98304]{2,1,0:T(2,128)(2,1)}, u32[]{:S(2)}, u32[]{:S(2)}) async-start(bf16[16,2,98304]{2,1,0:T(2,128)(2,1)} %reshape.156), calls=%async_computation.1 | async-start | bytes 12582912 | tf_op jit(solution)/shard_map/all_to_all | solution.py:103
  92.0 99.0 %all-gather.2.cloned.1.call-start = ((), (), s32[]{:S(2)}) async-start(), calls=%async_computation.4 | async-start | bytes 1114112 | tf_op jit(solution)/shard_map/all_gather | solution.py:98
  203.4 25.6 %copy-start.1 = (f32[256]{0:T(256)S(1)}, f32[256]{0:T(256)}, u32[]{:S(2)}) copy-start(f32[256]{0:T(256)} %param.16) | copy-start | bytes 3076
  401.5 142.2 %all-to-all-start.2 = ((bf16[16,2,98304]{2,1,0:T(2,128)(2,1)}), bf16[16,2,98304]{2,1,0:T(2,128)(2,1)}, u32[]{:S(2)}, u32[]{:S(2)}) async-start(bf16[16,2,98304]{2,1,0:T(2,128)(2,1)} %reshape.158), calls=%async_computation.2 | async-start | bytes 12582912 | tf_op jit(solution)/shard_map/all_to_all | solution.py:116
  429.5 276.4 %all-reduce.3.cloned.1.call-start = ((), (), s32[]{:S(2)}) async-start(), calls=%async_computation.5 | async-start | bytes 262144 | tf_op jit(solution)/shard_map/psum | solution.py:126
  595.3 221.8 %reduce-scatter.2.cloned.1.call-start = ((), (), s32[]{:S(2)}) async-start(), calls=%async_computation.6 | async-start | bytes 8912896 | tf_op jit(solution)/shard_map/reduce_scatter | solution.py:125
Sparse Core Ops, SparseCore 0:
  95.0 95.9 all-gather.1
  595.4 110.4 all-reduce.2
  710.5 106.4 reduce-scatter.1
where the time goes:
time: 830 us; the launch traced here: 825 us
  waiting for transfers between devices  377 us (45%)
  local copies, waits for them, and re-layouts  186 us (22%)
  matrix products  124 us (15%)
  blocking collectives  56.7 us (7%)
  starting transfers between devices  42.1 us (5%)
  other arithmetic  21.9 us (3%)
  between operations  15.7 us (2%)
    all_to_all x1, waiting for transfers between devices, local(): lax.all_to_all(d_blocks.reshape(n_dev, capacity, 2, orbitals, orbitals),...  114 us
    reduce_scatter x1, waiting for transfers between devices, local(): lax.psum_scatter(term_second, 'blk', scatter_dimension=1, tiled=True)  109 us
    all_gather x1, waiting for transfers between devices, local(): whole_panel = lax.all_gather(panel, 'blk', axis=0, tiled=True)  98 us
    unnamed x10, local copies, waits for them, and re-layouts  68.4 us
    psum x1, blocking collectives, local(): lax.psum((term_first, jnp.sum(residual * residual)), 'blk')  56.7 us
    psum x1, waiting for transfers between devices, local(): lax.psum((term_first, jnp.sum(residual * residual)), 'blk')  45.8 us
    all_to_all x1, starting transfers between devices, local(): lax.all_to_all(d_blocks.reshape(n_dev, capacity, 2, orbitals, orbitals),...  28 us
    dot_general x12, matrix products, forward(): jnp.einsum('rs,sap->rap', selector, contrib, precision=lax.Precision.HIGH...  26.3 us
  transfers between devices with their start and end apart: 6, of which 5 were waited for; matrix products, arithmetic and copies ran while one was open for 10% of the time, Pallas kernels for 0%

commit v1 on v0

--- a/solution.py
+++ b/solution.py
@@ -95,7 +95,29 @@
     rows_sent = jnp.concatenate([pair_row, empty_label])[source]
     cols_sent = jnp.concatenate([my_index * blk_dev + pair_col, jnp.zeros((1,), jnp.int32)])[source]
     labels = jnp.stack([rows_sent, cols_sent], axis=-1).reshape(n_dev, capacity, 2)
-    whole_panel = lax.all_gather(panel, "blk", axis=0, tiled=True)
+    answer, mixed_arr, local_next = (
+        jax.lax.axis_size("blk"),
+        jax.lax.axis_index("blk"),
+        panel.shape[0],
+    )
+    xs_all = tuple(((w, (w + 1) % answer) for w in range(answer)))
+    lanes = tuple(((w, (w - 1) % answer) for w in range(answer)))
+    whole_panel = jnp.zeros((*panel.shape[:0], answer * local_next, *panel.shape[1:]), panel.dtype)
+    whole_panel = lax.dynamic_update_slice_in_dim(
+        whole_panel, panel, mixed_arr * local_next, axis=0
+    )
+    tile_out = inter = panel
+    base_arr = answer // 2
+    for ii in range(1, base_arr + 1):
+        tile_out = jax.lax.ppermute(tile_out, "blk", xs_all)
+        whole_panel = lax.dynamic_update_slice_in_dim(
+            whole_panel, tile_out, (mixed_arr - ii) % answer * local_next, axis=0
+        )
+        if ii < answer - base_arr:
+            inter = jax.lax.ppermute(inter, "blk", lanes)
+            whole_panel = lax.dynamic_update_slice_in_dim(
+                whole_panel, inter, (mixed_arr + ii) % answer * local_next, axis=0
+            )
     pre, hidden, blocks = predict(features, w_first, w_second, orbitals)
     padded = jnp.concatenate([blocks, jnp.zeros((1, blocks.shape[1]), jnp.bfloat16)], axis=0)
     send_blocks = padded[source].reshape(n_dev, capacity, 2, orbitals, orbitals)

time: 830 us -> 868 us (1.046)
  starting transfers between devices: 42.1 us -> 68.8 us
  waiting for transfers between devices: 377 us -> 388 us
    ppermute x0 -> x15, waiting for transfers between devices: none -> 119 us  [the longest x8 119 us: local(): tile_out = jax.lax.ppermute(tile_out, 'blk', xs_all)]
    all_gather x1 -> x0, waiting for transfers between devices: 98 us -> none  [local(): whole_panel = lax.all_gather(panel, 'blk', axis=0, tiled=True)]
    ppermute x0 -> x15, starting transfers between devices: none -> 33.6 us  [the longest x7 31 us: local(): inter = jax.lax.ppermute(inter, 'blk', lanes)]
    all_to_all x1, waiting for transfers between devices: 9.16 us -> 0.01 us  [local(): lax.all_to_all(send_blocks, 'blk', split_axis=0, concat_axis=0, tiled=True)]
    unnamed x10 -> x12, local copies, waits for them, and re-layouts: 68.4 us -> 68.4 us
  transfers between devices with their start and end apart: 6 -> 20, of which waited for: 5 -> 12; matrix products, arithmetic and copies ran while one was open for 10% -> 9% of each run, Pallas kernels for 0% -> 0%
where the time goes in v1:
time: 868 us; the launch traced here: 862 us
  waiting for transfers between devices  388 us (45%)
  local copies, waits for them, and re-layouts  185 us (21%)
  matrix products  124 us (14%)
  starting transfers between devices  68.8 us (8%)
  blocking collectives  56.7 us (7%)
  other arithmetic  21.8 us (3%)
  between operations  16.1 us (2%)
    ppermute x8, waiting for transfers between devices, local(): tile_out = jax.lax.ppermute(tile_out, 'blk', xs_all)  119 us
    all_to_all x1, waiting for transfers between devices, local(): lax.all_to_all(d_blocks.reshape(n_dev, capacity, 2, orbitals, orbitals),...  114 us
    reduce_scatter x1, waiting for transfers between devices, local(): lax.psum_scatter(term_second, 'blk', scatter_dimension=1, tiled=True)  110 us
    unnamed x12, local copies, waits for them, and re-layouts  68.4 us
    psum x1, blocking collectives, local(): lax.psum((term_first, jnp.sum(residual * residual)), 'blk')  56.7 us
    psum x1, waiting for transfers between devices, local(): lax.psum((term_first, jnp.sum(residual * residual)), 'blk')  45.7 us
    ppermute x7, starting transfers between devices, local(): inter = jax.lax.ppermute(inter, 'blk', lanes)  31 us
    dot_general x12, matrix products, forward(): jnp.einsum('rs,sap->rap', selector, contrib, precision=lax.Precision.HIGH...  26.3 us
  transfers between devices with their start and end apart: 20, of which 12 were waited for; matrix products, arithmetic and copies ran while one was open for 9% of the time, Pallas kernels for 0%

profile of v1, /device:TPU:0, one launch (start us, length us, event | category | flops | bytes accessed | tf_op | source)
XLA Modules:
  0.0 862.4 jit_solution(5082843586348704089)
XLA Ops:
  19.4 7.4 all-to-all-start
  33.7 17.6 %gather_fusion.4 = bf16[384,8192]{1,0:T(8,128)(2,1)} fusion(bf16[257,8192]{1,0:T(8,128)(2,1)} %concatenate.12, s32[1024]{0:T(1024)S(1)} %pad_clamp_fusion.3), kind=kCustom, calls=%fused_computation.4 | custom fusion | bytes 12584448 | tf_op jit(solution)/shard_map/gather | solution.py:123
  51.3 17.9 %reshape.77 = bf16[16,24,2,64,64]{4,3,2,1,0:T(8,128)(2,1)} reshape(bf16[384,8192]{1,0:T(8,128)(2,1)} %gather_fusion.4) | data formatting | bytes 12582912 | tf_op jit(solution)/shard_map/reshape | solution.py:123
  69.2 16.7 %reshape.156 = bf16[16,2,98304]{2,1,0:T(2,128)(2,1)} reshape(bf16[16,24,2,64,64]{4,3,2,1,0:T(8,128)(2,1)} %reshape.77) | data formatting | bytes 12582912
  85.9 6.2 all-to-all-start.1
  96.9 103.2 %collective-permute-done = bf16[2,64,256]{2,1,0:T(8,128)(2,1)S(1)} collective-permute-done((bf16[2,64,256]{2,1,0:T(8,128)(2,1)S(1)}, bf16[2,64,256]{2,1,0:T(8,128)(2,1)S(1)}, u32[]{:S(2)}, u32[]{:S(2)}) %collective-permute-start) | collective-permute-done | bytes 65568 | tf_op jit(solution)/shard_map/ppermute | solution.py:112
  219.8 4.4 collective-permute-start.9
  226.3 4.5 collective-permute-start.11
  232.8 4.6 collective-permute-start.13
  245.6 11.2 %gather_fusion.5 = bf16[384,64,256]{2,1,0:T(8,128)(2,1)} fusion(bf16[32,64,256]{2,1,0:T(8,128)(2,1)S(1)} %constant_dynamic-update-slice_fusion, s32[1024]{0:T(1024)S(1)} %pad_clamp_fusion.2), kind=kCustom, calls=%fused_computation.5 | custom fusion | bytes 25167360 | tf_op jit(solution)/shard_map/gather | solution.py:129
  256.8 16.4 %reshape.157 = bf16[16,24,2,64,64]{4,3,2,1,0:T(8,128)(2,1)} reshape(bf16[16,2,98304]{2,1,0:T(2,128)(2,1)} %all-to-all-done.1) | data formatting | bytes 12582912
  273.2 82.3 %while.22 = (s32[]{:T(128)}, f32[2,64,256]{2,0,1:T(2,128)S(1)}, s32[12,32]{1,0:T(8,128)S(1)}, bf16[12,32,2,64,64]{4,3,2,1,0:T(8,128)(2,1)}, bf16[12,32,64,256]{3...) while((s32[]{:T(128)}, f32[2,64,256]{2,0,1:T(2,128)S(1)}, ...), condition=%wide.region_5.6_spmd.clone, body=%wide.region_4.5_spmd.clone.sunk | while | flops 147914816 | bytes 13372387 | solution.py:55
  356.2 72.8 %while.21 = (s32[]{:T(128)}, bf16[12,32,2,64,64]{4,3,2,1,0:T(8,128)(2,1)}, s32[12,32]{1,0:T(8,128)S(1)}, bf16[2,64,256]{2,1,0:T(8,128)(2,1)S(1)}, bf16[12,32,64,...) while((s32[]{:T(128)}, bf16[12,32,2,64,64]{4,3,2,1,0:T(8,128)(2,1)}, ...), condition=%wide.region_9.10_spmd, body=%wide.region_8.9_spmd.sunk | while | flops 135791680 | bytes 10492341 | solution.py:73
  429.0 16.6 %reshape.158 = bf16[16,2,98304]{2,1,0:T(2,128)(2,1)} reshape(bf16[16,24,2,64,64]{4,3,2,1,0:T(8,128)(2,1)} %bitcast.100) | data formatting | bytes 12582912
  445.6 21.3 %all-to-all-start.2 = ((bf16[16,2,98304]{2,1,0:T(2,128)(2,1)}), bf16[16,2,98304]{2,1,0:T(2,128)(2,1)}, u32[]{:S(2)}, u32[]{:S(2)}) async-start(bf16[16,2,98304]{2,1,0:T(2,128)(2,1)} %reshape.158), calls=%async_computation.2 | async-start | bytes 12582912 | tf_op jit(solution)/shard_map/all_to_all | solution.py:138
  467.3 113.9 %all-to-all-done.2 = bf16[16,2,98304]{2,1,0:T(2,128)(2,1)} async-done(((bf16[16,2,98304]{2,1,0:T(2,128)(2,1)}), bf16[16,2,98304]{2,1,0:T(2,128)(2,1)}, u32[]{:S(2)}, u32[]{:S(2)}) %all-to-all-start.2) | async-done | bytes 6291488 | tf_op jit(solution)/shard_map/all_to_all | solution.py:138
  581.2 16.3 %reshape.159 = bf16[16,24,2,64,64]{4,3,2,1,0:T(8,128)(2,1)} reshape(bf16[16,2,98304]{2,1,0:T(2,128)(2,1)} %all-to-all-done.2) | data formatting | bytes 12582912
  597.5 17.0 %reshape.80 = bf16[384,8192]{1,0:T(8,128)(2,1)} reshape(bf16[16,24,2,64,64]{4,3,2,1,0:T(8,128)(2,1)} %reshape.159) | data formatting | bytes 12582912 | tf_op jit(solution)/shard_map/reshape | solution.py:145
  614.5 12.5 %gather_fusion.6 = bf16[256,8192]{1,0:T(8,128)(2,1)} fusion(bf16[384,8192]{1,0:T(8,128)(2,1)} %reshape.80, s32[1024]{0:T(1024)S(1)} %pad_clamp_fusion.1), kind=kCustom, calls=%fused_computation.6 | custom fusion | bytes 8389632 | tf_op jit(solution)/shard_map/gather | solution.py:145
  627.0 5.7 convolution_bitcast_fusion
  632.8 6.7 convolution_multiply_fusion
  639.5 56.7 %psum.14 = f32[]{:T(128)} all-reduce(f32[]{:T(128)} %get-tuple-element.172), channel_id=1, replica_groups=mesh['parts'=2,'blk'=16] {'blk'}, use_global_device_ids=true, to_apply=%region_7.8 | all-reduce | flops 1 | bytes 8 | tf_op jit(solution)/shard_map/psum | solution.py:148
  697.5 45.7 %all-reduce.3.cloned.1.call-done = f32[128,256]{0,1:T(8,128)} async-done(((f32[128,256]{0,1:T(8,128)}), f32[128,256]{0,1:T(8,128)}) %all-reduce.3.cloned.1.call-update) | async-done | bytes 131088 | tf_op jit(solution)/shard_map/psum | solution.py:148
  744.9 109.5 %reduce-scatter.2.cloned.1.call-done = f32[256,512]{1,0:T(8,128)} async-done(((f32[256,8192]{1,0:T(8,128)}), f32[256,512]{1,0:T(8,128)}) %reduce-scatter.2.cloned.1.call-update) | async-done | bytes 524304 | tf_op jit(solution)/shard_map/reduce_scatter | solution.py:147
  (246 shorter events, 213.2 us)
Async XLA Ops:
  7.2 19.6 %copy-start = (bf16[256,128]{1,0:T(8,128)(2,1)S(1)}, bf16[256,128]{1,0:T(8,128)(2,1)}, u32[]{:S(2)}) copy-start(bf16[256,128]{1,0:T(8,128)(2,1)} %param.12) | copy-start | bytes 196612
  19.4 66.5 %all-to-all-start = ((s32[16,24,2]{1,2,0:T(2,128)}), s32[16,24,2]{1,2,0:T(2,128)S(1)}, u32[]{:S(2)}, u32[]{:S(2)}) async-start(s32[16,24,2]{1,2,0:T(2,128)} %pad_add_fusion), calls=%async_computation | async-start | bytes 32768 | tf_op jit(solution)/shard_map/all_to_all | solution.py:126
  85.9 6.2 copy-start.1
  85.9 170.8 %all-to-all-start.1 = ((bf16[16,2,98304]{2,1,0:T(2,128)(2,1)}), bf16[16,2,98304]{2,1,0:T(2,128)(2,1)}, u32[]{:S(2)}, u32[]{:S(2)}) async-start(bf16[16,2,98304]{2,1,0:T(2,128)(2,1)} %reshape.156), calls=%async_computation.1 | async-start | bytes 12582912 | tf_op jit(solution)/shard_map/all_to_all | solution.py:125
  92.1 108.0 %collective-permute-start = (bf16[2,64,256]{2,1,0:T(8,128)(2,1)S(1)}, bf16[2,64,256]{2,1,0:T(8,128)(2,1)S(1)}, u32[]{:S(2)}, u32[]{:S(2)}) collective-permute-start(bf16[2,64,256]{2,1,0:T(8,128)(2,1)S(1)} %copy-done.1), channel_id=1, source_target_pairs={{0,1},{1,2},{2,3},{3,4},{4,5},{5,6},{6,7},{7,8},{8,9},{9,10},{10,1... | collective-permute-start | bytes 196616 | tf_op jit(solution)/shard_map/ppermute | solution.py:112
  92.5 107.6 %collective-permute-start.1 = (bf16[2,64,256]{2,1,0:T(8,128)(2,1)S(1)}, bf16[2,64,256]{2,1,0:T(8,128)(2,1)S(1)}, u32[]{:S(2)}, u32[]{:S(2)}) collective-permute-start(bf16[2,64,256]{2,1,0:T(8,128)(2,1)S(1)} %copy-done.1), channel_id=1, source_target_pairs={{0,15},{1,0},{2,1},{3,2},{4,3},{5,4},{6,5},{7,6},{8,7},{9,8},{10,9... | collective-permute-start | bytes 196616 | tf_op jit(solution)/shard_map/ppermute | solution.py:117
  200.1 6.6 collective-permute-start.2
  200.1 6.6 collective-permute-start.3
  206.7 6.5 collective-permute-start.4
  206.7 6.5 collective-permute-start.5
  213.2 6.5 collective-permute-start.6
  213.2 6.5 collective-permute-start.7
  219.8 6.5 collective-permute-start.8
  219.8 6.5 collective-permute-start.9
  226.3 6.5 collective-permute-start.10
  226.3 6.5 collective-permute-start.11
  232.8 6.4 collective-permute-start.12
  232.8 9.1 %collective-permute-start.13 = (bf16[2,64,256]{2,1,0:T(8,128)(2,1)S(1)}, bf16[2,64,256]{2,1,0:T(8,128)(2,1)S(1)}, u32[]{:S(2)}, u32[]{:S(2)}) collective-permute-start(bf16[2,64,256]{2,1,0:T(8,128)(2,1)S(1)} %collective-permute-done.11), channel_id=1, source_target_pairs={{0,15},{1,0},{2,1},{3,2},{4,3},{5,4},{6,5},{7,6},{8,7},{9,8},{10,9... | collective-permute-start | bytes 196616 | tf_op jit(solution)/shard_map/ppermute | solution.py:117
  239.1 6.4 collective-permute-start.14
  256.7 16.4 %copy-start.2 = (f32[256]{0:T(256)S(1)}, f32[256]{0:T(256)}, u32[]{:S(2)}) copy-start(f32[256]{0:T(256)} %param.16) | copy-start | bytes 3076
  445.6 135.5 %all-to-all-start.2 = ((bf16[16,2,98304]{2,1,0:T(2,128)(2,1)}), bf16[16,2,98304]{2,1,0:T(2,128)(2,1)}, u32[]{:S(2)}, u32[]{:S(2)}) async-start(bf16[16,2,98304]{2,1,0:T(2,128)(2,1)} %reshape.158), calls=%async_computation.2 | async-start | bytes 12582912 | tf_op jit(solution)/shard_map/all_to_all | solution.py:138
  467.0 276.3 %all-reduce.3.cloned.1.call-start = ((), (), s32[]{:S(2)}) async-start(), calls=%async_computation.4 | async-start | bytes 262144 | tf_op jit(solution)/shard_map/psum | solution.py:148
  632.7 221.7 %reduce-scatter.2.cloned.1.call-start = ((), (), s32[]{:S(2)}) async-start(), calls=%async_computation.5 | async-start | bytes 8912896 | tf_op jit(solution)/shard_map/reduce_scatter | solution.py:147
Sparse Core Ops, SparseCore 0:
  632.8 110.3 all-reduce.2
  747.9 106.4 reduce-scatter.1
